TPU v7x, 512 devices: a whole 4x4x16 slice. The times are simulated.
512 devices in a mesh: fsdp: 64 (over x, z), tensor: 8 (over y, core).
Axes of the slice: x: 4, y: 4, z: 16, core: 2. Of those that a mesh axis runs over, the one named last changes fastest.
Arguments:
- gate_pre: bfloat16 [12288, 14336], P(('fsdp', 'tensor')), may hold values from -6 to 6
- up_pre: bfloat16 [12288, 14336], P(('fsdp', 'tensor')), may hold values from -6 to 6
- cotangent: bfloat16 [12288, 4096], P('fsdp'), may hold values from -6 to 6
- w_slots: bfloat16 [8, 192, 128, 128], P('tensor', 'fsdp'), may hold values from -0.15625 to 0.15625
- slot_ids: int32 [8, 192], P('tensor'), may hold values from -1 to 447, as said below
Outputs:
- d_gate: bfloat16 [12288, 14336], P(('fsdp', 'tensor'))
- d_up: bfloat16 [12288, 14336], P(('fsdp', 'tensor'))
- w_grad: float32 [8, 192, 128, 128], P('tensor', 'fsdp')
Inputs may be any that keep to these rules, and one draw needn't show every extreme that they name: `slot_ids`: in row t, slots s * 3 to s * 3 + 2 list the kept blocks owned by fsdp index s in tensor slice t as local row block * 32 + column block, filling the first slots and -1 in the rest; every owner has 2 or 3 kept blocks, some owner of every row exactly 3 and some exactly 2; no block id appears twice in a row.
All inputs are finite; a program needn't handle non-finite values.
Results may differ from a plain program's by a relative error of at most 0.0085.
Values may be sent and summed in bfloat16 or wider, within the bound.
No kernel may reach another device: no remote copies, remote signals or barrier semaphores. Data moves between devices by JAX's collectives and lax.ppermute only.
A program may use at most 128 MiB of HBM per device.

v0:
```python
import math
import jax
import jax.numpy as jnp
from jax import lax
from jax.sharding import PartitionSpec as P


def swiglu_value(gate_part, up_part):
    gate_f = gate_part.astype(jnp.float32)
    gate_sig = jax.nn.sigmoid(gate_f)
    return (gate_f * gate_sig * up_part.astype(jnp.float32)).astype(jnp.bfloat16)


def swiglu_grads(dh_part, gate_part, up_part):
    gate_f = gate_part.astype(jnp.float32)
    up_f = up_part.astype(jnp.float32)
    gate_sig = jax.nn.sigmoid(gate_f)
    dh_f = dh_part.astype(jnp.float32)
    grad_gate = (dh_f * up_f * (gate_sig * (1.0 + gate_f * (1.0 - gate_sig)))).astype(jnp.bfloat16)
    grad_up = (dh_f * (gate_f * gate_sig)).astype(jnp.bfloat16)
    return (grad_gate, grad_up)


def body(gate_pre, up_pre, cotangent, w_slots, slot_ids):
    n_fsdp = lax.axis_size("fsdp")
    block_size = w_slots.shape[2]
    token_count = cotangent.shape[0]
    model_width = cotangent.shape[1]
    col_count = model_width // block_size
    ff_dev = gate_pre.shape[1] // lax.axis_size("tensor")
    row_count = ff_dev // block_size
    slot_total = slot_ids.shape[1]
    cap_local = w_slots.shape[1]
    slot_list = slot_ids[0]
    usable = slot_list >= 0
    safe_ids = jnp.maximum(slot_list, 0)
    row_index = jnp.where(usable, safe_ids // col_count, row_count)
    col_index = safe_ids % col_count
    row_clip = jnp.minimum(row_index, row_count - 1)
    usable_f = usable.astype(jnp.float32)
    row_range = jnp.arange(row_count, dtype=jnp.int32)
    dy_blocks = cotangent.reshape(token_count, col_count, block_size)
    gate_t, up_t = (
        lax.all_to_all(gate_pre, "tensor", split_axis=1, concat_axis=0, tiled=True),
        lax.all_to_all(up_pre, "tensor", split_axis=1, concat_axis=0, tiled=True),
    )
    hidden = swiglu_value(gate_t, up_t)
    start_sum = jnp.zeros((token_count, row_count, block_size), jnp.float32)
    running = start_sum
    shard_piece = lax.all_gather(w_slots, "fsdp", axis=1, tiled=True)
    slot_count = shard_piece.shape[1]
    sub_size = math.gcd(slot_count, 48)
    rows_part = row_index.reshape(slot_count // sub_size, sub_size)
    cols_part = col_index.reshape(slot_count // sub_size, sub_size)
    weight_part = shard_piece[0].reshape(slot_count // sub_size, sub_size, block_size, block_size)

    def advance(carried, packed_item):
        rows_now, cols_now, weight_now = packed_item
        dy_picked = jnp.take(dy_blocks, cols_now, axis=1)
        contrib = jnp.einsum(
            "tsb,sab->tsa", dy_picked, weight_now, preferred_element_type=jnp.float32
        )
        onehot = (rows_now[:, None] == row_range[None, :]).astype(jnp.float32)
        added = jnp.einsum("tsa,sr->tra", contrib, onehot, precision=lax.Precision.HIGHEST)
        return (carried + added, None)

    running, _ = lax.scan(advance, running, (rows_part, cols_part, weight_part))
    d_hidden = running.reshape(token_count, ff_dev).astype(jnp.bfloat16)
    grad_scale = 1.0 / math.sqrt(token_count * n_fsdp)
    hidden_blocks = hidden.reshape(token_count, row_count, block_size)
    group_size = math.gcd(slot_total, 48)
    group_count = slot_total // group_size

    def partial_group(packed_item):
        rows_now, cols_now, scale_now = packed_item
        h_picked = jnp.take(hidden_blocks, rows_now, axis=1)
        dy_picked = jnp.take(dy_blocks, cols_now, axis=1)
        product = jnp.einsum(
            "tsa,tsb->sab", h_picked, dy_picked, preferred_element_type=jnp.float32
        )
        return (product * scale_now[:, None, None]).astype(jnp.bfloat16)

    partials = lax.map(
        partial_group,
        (
            row_clip.reshape(group_count, group_size),
            col_index.reshape(group_count, group_size),
            (grad_scale * usable_f).reshape(group_count, group_size),
        ),
    )
    partials = partials.reshape(slot_total, block_size, block_size)
    arrived = lax.all_to_all(partials, "fsdp", split_axis=0, concat_axis=0, tiled=True)
    w_grad = (
        arrived.astype(jnp.float32)
        .reshape(n_fsdp, cap_local, block_size, block_size)
        .sum(axis=0)[None]
    )
    grad_gate_t, grad_up_t = swiglu_grads(d_hidden, gate_t, up_t)
    d_gate, d_up = (
        lax.all_to_all(grad_gate_t, "tensor", split_axis=0, concat_axis=1, tiled=True),
        lax.all_to_all(grad_up_t, "tensor", split_axis=0, concat_axis=1, tiled=True),
    )
    return (d_gate, d_up, w_grad)


def solution(mesh):
    placed = (
        P(("fsdp", "tensor"), None),
        P(("fsdp", "tensor"), None),
        P("fsdp", None),
        P("tensor", "fsdp", None, None),
        P("tensor", None),
    )
    return jax.shard_map(
        body,
        mesh=mesh,
        in_specs=placed,
        out_specs=(
            P(("fsdp", "tensor"), None),
            P(("fsdp", "tensor"), None),
            P("tensor", "fsdp", None, None),
        ),
        check_vma=False,
    )
```

profile of v0, /device:TPU:8, one launch (start us, length us, event | category | flops | bytes accessed | tf_op | source)
XLA Modules:
  0.0 586.6 jit_solution(15510980413584426776)
XLA Ops:
  7.2 0.0 copy-start
  7.2 0.0 all-gather.2.cloned.1.call-start
  7.2 0.7 all-gather.2.cloned.1.call-update
  7.9 2.0 copy.45
  9.9 9.9 %all-to-all-start = ((bf16[24,8,1792]{2,0,1:T(8,128)(2,1)}), bf16[24,8,1792]{2,0,1:T(8,128)(2,1)}, u32[]{:S(2)}, u32[]{:S(2)}) async-start(bf16[24,8,1792]{2,0,1:T(8,128)(2,1)} %bitcast.85), calls=%async_computation | async-start | bytes 1376256 | tf_op jit(solution)/shard_map/all_to_all | solution.py:45
  19.8 0.0 copy-done.4
  19.8 0.1 ne.31
  19.9 0.1 ge.24
  20.0 0.1 rem.19
  20.1 0.1 div.21
  20.2 0.9 copy.44
  21.1 0.4 copy_bitcast_fusion
  21.6 9.0 %all-to-all-done = bf16[24,8,1792]{2,0,1:T(8,128)(2,1)} async-done(((bf16[24,8,1792]{2,0,1:T(8,128)(2,1)}), bf16[24,8,1792]{2,0,1:T(8,128)(2,1)}, u32[]{:S(2)}, u32[]{:S(2)}) %all-to-all-start) | async-done | bytes 688160 | tf_op jit(solution)/shard_map/all_to_all | solution.py:45
  30.6 5.5 all-to-all-start.1
  36.1 2.3 convert_bitcast_fusion.1
  38.4 127.6 %all-gather.2.cloned.1.call-done = bf16[1,192,128,128]{3,2,0,1:T(8,128)(2,1)} async-done(((bf16[1,3,128,128]{3,2,0,1:T(8,128)(2,1)}), bf16[1,192,128,128]{3,2,0,1:T(8,128)(2,1)}) %all-gather.2.cloned.1.call-update) | async-done | bytes 6291472 | tf_op jit(solution)/shard_map/all_gather | solution.py:50
  166.0 46.6 %while.22 = (s32[]{:T(128)}, f32[192,14,128]{2,1,0:T(8,128)}, s32[4,48]{1,0:T(4,128)S(1)}, bf16[4,48,128,128]{3,2,1,0:T(8,128)(2,1)}, s32[4,48]{1,0:T(4,128)S(1)...) while((s32[]{:T(128)}, f32[192,14,128]{2,1,0:T(8,128)}, s32[4,48]{1,0:T(4,128)S(1)}, ...), condition=%wide.region_1.3_spmd.clone, body=%wide.region_0.2_spmd.clone.sunk | while | flops 502040512 | bytes 31856200 | solution.py:67
  166.1 2.3 gather_fusion.2
  168.4 3.4 fusion.64
  171.8 4.7 bitcast_add_fusion.2
  176.5 1.2 copy-done.2
  177.7 2.3 gather_fusion.2
  180.0 3.4 fusion.64
  183.5 4.7 bitcast_add_fusion.2
  188.2 1.2 copy-done.2
  189.4 2.3 gather_fusion.2
  191.7 3.4 fusion.64
  195.1 4.7 bitcast_add_fusion.2
  199.8 1.2 copy-done.2
  201.0 2.3 gather_fusion.2
  203.3 3.4 fusion.64
  206.8 4.7 bitcast_add_fusion.2
  211.5 1.2 copy-done.2
  212.6 2.7 convert_convert_fusion
  215.3 2.6 reshape.111
  217.9 0.0 all-to-all-done.1
  217.9 3.5 multiply_convert_fusion.2
  221.4 5.0 all-to-all-start.3
  226.4 2.3 convert_bitcast_fusion
  228.7 2.6 reshape.113
  231.3 2.7 reshape.112
  234.0 2.3 multiply_convert_fusion.1
  236.3 1.0 copy.30
  237.3 0.0 all-to-all-done.3
  237.3 5.4 all-to-all-start.2
  242.7 43.6 %while.21 = (s32[]{:T(128)}, bf16[4,48,128,128]{3,2,1,0:T(8,128)(2,1)}, s32[4,48]{1,0:T(4,128)S(1)}, bf16[192,14,128]{2,0,1:T(8,128)(2,1)}, s32[4,48]{1,0:T(4,12...) while((s32[]{:T(128)}, bf16[4,48,128,128]{3,2,1,0:T(8,128)(2,1)}, ...), condition=%wide.region_3.5_spmd, body=%wide.region_2.4_spmd.sunk | while | flops 305924832 | bytes 15739437 | solution.py:83
  242.8 3.5 gather_fusion.1
  246.3 2.4 gather_fusion
  248.7 4.9 bitcast_dynamic-update-slice_fusion.2
  253.7 3.5 gather_fusion.1
  257.2 2.4 gather_fusion
  259.6 4.9 bitcast_dynamic-update-slice_fusion.2
  264.5 3.5 gather_fusion.1
  268.0 2.4 gather_fusion
  270.4 4.9 bitcast_dynamic-update-slice_fusion.2
  275.4 3.5 gather_fusion.1
  278.9 2.4 gather_fusion
  281.3 4.9 bitcast_dynamic-update-slice_fusion.2
  286.3 0.0 all-to-all-done.2
  286.3 9.7 %all-to-all-start.4 = ((bf16[192,128,128]{2,1,0:T(8,128)(2,1)}), bf16[192,128,128]{2,1,0:T(8,128)(2,1)}, u32[]{:S(2)}, u32[]{:S(2)}) async-start(bf16[192,128,128]{2,1,0:T(8,128)(2,1)} %bitcast.111), calls=%async_computation.4 | async-start | bytes 12582912 | tf_op jit(solution)/shard_map/all_to_all | solution.py:92
  295.9 2.0 copy.36
  297.9 2.0 copy.35
  299.9 275.3 %all-to-all-done.4 = bf16[192,128,128]{2,1,0:T(8,128)(2,1)} async-done(((bf16[192,128,128]{2,1,0:T(8,128)(2,1)}), bf16[192,128,128]{2,1,0:T(8,128)(2,1)}, u32[]{:S(2)}, u32[]{:S(2)}) %all-to-all-start.4) | async-done | bytes 6291488 | tf_op jit(solution)/shard_map/all_to_all | solution.py:92
  575.2 4.6 convert_reduce_fusion
  (54 shorter events, 0.3 us)
Async XLA Ops:
  7.2 14.0 %copy-start = (bf16[192,4096]{1,0:T(8,128)(2,1)S(1)}, bf16[192,4096]{1,0:T(8,128)(2,1)}, u32[]{:S(2)}) copy-start(bf16[192,4096]{1,0:T(8,128)(2,1)} %param.13) | copy-start | bytes 4718596
  7.2 12.6 %copy-start.4 = (s32[1,192]{1,0:T(1,128)S(1)}, s32[1,192]{1,0:T(1,128)}, u32[]{:S(2)}) copy-start(s32[1,192]{1,0:T(1,128)} %param.15) | copy-start | bytes 2308
  7.2 13.0 %copy-start.3 = (bf16[24,14336]{1,0:T(8,128)(2,1)S(1)}, bf16[24,14336]{1,0:T(8,128)(2,1)}, u32[]{:S(2)}) copy-start(bf16[24,14336]{1,0:T(8,128)(2,1)} %param.11) | copy-start | bytes 2064388
  7.2 158.8 %all-gather.2.cloned.1.call-start = ((), (), s32[]{:S(2)}) async-start(), calls=%async_computation.5 | async-start | bytes 6389760 | tf_op jit(solution)/shard_map/all_gather | solution.py:50
  9.9 20.6 %all-to-all-start = ((bf16[24,8,1792]{2,0,1:T(8,128)(2,1)}), bf16[24,8,1792]{2,0,1:T(8,128)(2,1)}, u32[]{:S(2)}, u32[]{:S(2)}) async-start(bf16[24,8,1792]{2,0,1:T(8,128)(2,1)} %bitcast.85), calls=%async_computation | async-start | bytes 1376256 | tf_op jit(solution)/shard_map/all_to_all | solution.py:45
  30.6 187.4 %all-to-all-start.1 = ((bf16[24,8,1792]{2,0,1:T(8,128)(2,1)}), bf16[24,8,1792]{2,0,1:T(8,128)(2,1)}, u32[]{:S(2)}, u32[]{:S(2)}) async-start(bf16[24,8,1792]{2,0,1:T(8,128)(2,1)} %bitcast.112), calls=%async_computation.1 | async-start | bytes 1376256 | tf_op jit(solution)/shard_map/all_to_all | solution.py:44
  168.4 3.4 copy-start.1
  176.5 1.2 copy-start.2
  180.0 3.4 copy-start.1
  188.2 1.2 copy-start.2
  191.7 3.4 copy-start.1
  199.8 1.2 copy-start.2
  203.3 3.4 copy-start.1
  211.5 1.2 copy-start.2
  221.4 15.9 %all-to-all-start.3 = ((bf16[8,24,1792]{2,1,0:T(8,128)(2,1)}), bf16[8,24,1792]{2,1,0:T(8,128)(2,1)}, u32[]{:S(2)}, u32[]{:S(2)}) async-start(bf16[8,24,1792]{2,1,0:T(8,128)(2,1)} %get-tuple-element.173), calls=%async_computation.3 | async-start | bytes 1376256 | tf_op jit(solution)/shard_map/all_to_all | solution.py:101
  237.3 48.9 %all-to-all-start.2 = ((bf16[8,24,1792]{2,1,0:T(8,128)(2,1)}), bf16[8,24,1792]{2,1,0:T(8,128)(2,1)}, u32[]{:S(2)}, u32[]{:S(2)}) async-start(bf16[8,24,1792]{2,1,0:T(8,128)(2,1)} %get-tuple-element.174), calls=%async_computation.2 | async-start | bytes 1376256 | tf_op jit(solution)/shard_map/all_to_all | solution.py:100
  286.3 288.9 %all-to-all-start.4 = ((bf16[192,128,128]{2,1,0:T(8,128)(2,1)}), bf16[192,128,128]{2,1,0:T(8,128)(2,1)}, u32[]{:S(2)}, u32[]{:S(2)}) async-start(bf16[192,128,128]{2,1,0:T(8,128)(2,1)} %bitcast.111), calls=%async_computation.4 | async-start | bytes 12582912 | tf_op jit(solution)/shard_map/all_to_all | solution.py:92
Sparse Core Ops, SparseCore 0:
  11.0 155.0 all-gather.1
where the time goes:
time: 588 us; the launch traced here: 587 us
  waiting for transfers between devices  413 us (70%)
  local copies, waits for them, and re-layouts  54.2 us (9%)
  matrix products  52.1 us (9%)
  starting transfers between devices  35.5 us (6%)
  other arithmetic  17.8 us (3%)
  between operations  14.1 us (2%)
    all_to_all x1, waiting for transfers between devices, body(): lax.all_to_all(partials, 'fsdp', split_axis=0, concat_axis=0, tiled=True)  275 us
    all_gather x1, waiting for transfers between devices, body(): shard_piece = lax.all_gather(w_slots, 'fsdp', axis=1, tiled=True)  128 us
    dot_general x4, matrix products, partial_group(): jnp.einsum('tsa,tsb->sab', h_picked, dy_picked, preferred_element_type=jn...  19.7 us
    dot_general x4, matrix products, advance(): jnp.einsum('tsa,sr->tra', contrib, onehot, precision=lax.Precision.HIGHEST)  18.7 us
    gather x4, local copies, waits for them, and re-layouts, partial_group(): h_picked = jnp.take(hidden_blocks, rows_now, axis=1)  14 us
    dot_general x4, matrix products, advance(): jnp.einsum('tsb,sab->tsa', dy_picked, weight_now, preferred_element_type=...  13.7 us
  transfers between devices with their start and end apart: 6, of which 3 were waited for; matrix products, arithmetic and copies ran while one was open for 19% of the time, Pallas kernels for 0%

commit v1 on v0

--- a/solution.py
+++ b/solution.py
@@ -3,6 +3,13 @@
 import jax.numpy as jnp
 from jax import lax
 from jax.sharding import PartitionSpec as P
+
+
+def part_the_lines(v0):
+    xs_all = []
+    for _ in range(jax.lax.axis_size("fsdp")):
+        xs_all.append(v0)
+    return jnp.concatenate(jax.lax.all_to_all(jnp.stack(xs_all, axis=0), "fsdp", 0, 0), axis=1)
 
 
 def swiglu_value(gate_part, up_part):
@@ -47,7 +54,7 @@
     hidden = swiglu_value(gate_t, up_t)
     start_sum = jnp.zeros((token_count, row_count, block_size), jnp.float32)
     running = start_sum
-    shard_piece = lax.all_gather(w_slots, "fsdp", axis=1, tiled=True)
+    shard_piece = part_the_lines(w_slots)
     slot_count = shard_piece.shape[1]
     sub_size = math.gcd(slot_count, 48)
     rows_part = row_index.reshape(slot_count // sub_size, sub_size)

time: 588 us -> 737 us (1.25)
  waiting for transfers between devices: 413 us -> 550 us
  blocking collectives: 0 us -> 19.6 us
  between operations: 14.1 us -> 0.74 us
    all_to_all x1, waiting for transfers between devices: 9 us -> 275 us  [part_the_lines(): jax.lax.all_to_all(jnp.stack(xs_all, axis=0), 'fsdp', 0, 0)]
    all_gather x1 -> x0, waiting for transfers between devices: 128 us -> none  [body(): shard_piece = lax.all_gather(w_slots, 'fsdp', axis=1, tiled=True)]
    all_to_all x0 -> x1, blocking collectives: none -> 19.6 us  [body(): lax.all_to_all(up_pre, 'tensor', split_axis=1, concat_axis=0, tiled=True)]
  transfers between devices with their start and end apart: 6 -> 5, of which waited for: 3 -> 2; matrix products, arithmetic and copies ran while one was open for 19% -> 15% of each run, Pallas kernels for 0% -> 0%
where the time goes in v1:
time: 737 us; the launch traced here: 736 us
  waiting for transfers between devices  550 us (75%)
  local copies, waits for them, and re-layouts  58.4 us (8%)
  matrix products  52.1 us (7%)
  starting transfers between devices  37.5 us (5%)
  blocking collectives  19.6 us (3%)
  other arithmetic  16.7 us (2%)
    all_to_all x1, waiting for transfers between devices, body(): lax.all_to_all(partials, 'fsdp', split_axis=0, concat_axis=0, tiled=True)  275 us
    all_to_all x1, waiting for transfers between devices, part_the_lines(): jax.lax.all_to_all(jnp.stack(xs_all, axis=0), 'fsdp', 0, 0)  275 us
    dot_general x4, matrix products, partial_group(): jnp.einsum('tsa,tsb->sab', h_picked, dy_picked, preferred_element_type=jn...  19.7 us
    all_to_all x1, blocking collectives, body(): lax.all_to_all(up_pre, 'tensor', split_axis=1, concat_axis=0, tiled=True)  19.6 us
    dot_general x4, matrix products, advance(): jnp.einsum('tsa,sr->tra', contrib, onehot, precision=lax.Precision.HIGHEST)  18.7 us
    all_to_all x1, starting transfers between devices, part_the_lines(): jax.lax.all_to_all(jnp.stack(xs_all, axis=0), 'fsdp', 0, 0)  14.8 us
  transfers between devices with their start and end apart: 5, of which 2 were waited for; matrix products, arithmetic and copies ran while one was open for 15% of the time, Pallas kernels for 0%

profile of v1, /device:TPU:8, one launch (start us, length us, event | category | flops | bytes accessed | tf_op | source)
XLA Modules:
  0.0 735.6 jit_solution(16821463487552826676)
XLA Ops:
  0.6 0.0 copy-start
  0.7 1.3 copy.44
  1.9 19.6 %all_to_all.68 = bf16[24,8,1792]{2,0,1:T(8,128)(2,1)} all-to-all(bf16[24,8,1792]{2,0,1:T(8,128)(2,1)S(1)} %bitcast.112), channel_id=1, replica_groups=mesh['fsdp'=64,'tensor'=8] {'tensor'}, dimensions={1} | all-to-all | bytes 1376256 | tf_op jit(solution)/shard_map/all_to_all | solution.py:52
  21.5 0.0 copy-done.5
  21.5 4.2 stack.2
  25.7 14.8 %all-to-all-start = ((bf16[64,1,3,128,128]{4,3,2,1,0:T(8,128)(2,1)}), bf16[64,1,3,128,128]{4,3,2,1,0:T(8,128)(2,1)}, u32[]{:S(2)}, u32[]{:S(2)}) async-start(bf16[64,1,3,128,128]{4,3,2,1,0:T(8,128)(2,1)} %stack.2), calls=%async_computation | async-start | bytes 12582912 | tf_op jit(solution)/shard_map/all_to_all | solution.py:12
  40.6 0.1 ne.31
  40.7 0.1 ge.24
  40.8 0.1 rem.19
  40.9 0.1 div.21
  41.0 0.9 copy.43
  41.9 0.4 copy_bitcast_fusion
  42.3 0.7 copy-done.3
  43.0 1.2 convert_bitcast_fusion.1
  44.2 274.9 %all-to-all-done = bf16[64,1,3,128,128]{4,3,2,1,0:T(8,128)(2,1)} async-done(((bf16[64,1,3,128,128]{4,3,2,1,0:T(8,128)(2,1)}), bf16[64,1,3,128,128]{4,3,2,1,0:T(8,128)(2,1)}, u32[]{:S(2)}, u32[]{:S(2)}) %all-to-all-start) | async-done | bytes 6291488 | tf_op jit(solution)/shard_map/all_to_all | solution.py:12
  319.1 5.6 all-to-all-start.2
  324.7 46.6 %while.22 = (s32[]{:T(128)}, f32[192,14,128]{2,1,0:T(8,128)}, s32[4,48]{1,0:T(4,128)S(1)}, bf16[4,48,128,128]{3,2,1,0:T(8,128)(2,1)}, s32[4,48]{1,0:T(4,128)S(1)...) while((s32[]{:T(128)}, f32[192,14,128]{2,1,0:T(8,128)}, s32[4,48]{1,0:T(4,128)S(1)}, ...), condition=%wide.region_1.3_spmd.clone, body=%wide.region_0.2_spmd.clone.sunk | while | flops 502040512 | bytes 31856200 | solution.py:74
  324.7 2.3 gather_fusion.2
  327.0 3.4 fusion.64
  330.5 4.7 bitcast_add_fusion.2
  335.1 1.2 copy-done.2
  336.4 2.3 gather_fusion.2
  338.7 3.4 fusion.64
  342.1 4.7 bitcast_add_fusion.2
  346.8 1.2 copy-done.2
  348.0 2.3 gather_fusion.2
  350.3 3.4 fusion.64
  353.8 4.7 bitcast_add_fusion.2
  358.5 1.2 copy-done.2
  359.7 2.3 gather_fusion.2
  362.0 3.4 fusion.64
  365.4 4.7 bitcast_add_fusion.2
  370.1 1.2 copy-done.2
  371.3 2.7 convert_convert_fusion
  374.0 2.6 reshape.114
  376.6 0.0 all-to-all-done.2
  376.6 3.5 multiply_convert_fusion.2
  380.1 4.8 all-to-all-start.4
  384.9 2.3 convert_bitcast_fusion
  387.2 2.6 reshape.116
  389.8 2.7 reshape.115
  392.4 2.3 multiply_convert_fusion.1
  394.7 1.0 copy.29
  395.8 0.0 all-to-all-done.4
  395.8 5.6 all-to-all-start.3
  401.3 43.6 %while.21 = (s32[]{:T(128)}, bf16[4,48,128,128]{3,2,1,0:T(8,128)(2,1)}, s32[4,48]{1,0:T(4,128)S(1)}, bf16[192,14,128]{2,0,1:T(8,128)(2,1)}, s32[4,48]{1,0:T(4,12...) while((s32[]{:T(128)}, bf16[4,48,128,128]{3,2,1,0:T(8,128)(2,1)}, ...), condition=%wide.region_3.5_spmd, body=%wide.region_2.4_spmd.sunk | while | flops 305924832 | bytes 15739437 | solution.py:90
  401.4 3.5 gather_fusion.1
  404.9 2.4 gather_fusion
  407.3 4.9 bitcast_dynamic-update-slice_fusion.2
  412.3 3.5 gather_fusion.1
  415.8 2.4 gather_fusion
  418.2 4.9 bitcast_dynamic-update-slice_fusion.2
  423.2 3.5 gather_fusion.1
  426.7 2.4 gather_fusion
  429.1 4.9 bitcast_dynamic-update-slice_fusion.2
  434.1 3.5 gather_fusion.1
  437.6 2.4 gather_fusion
  440.0 4.9 bitcast_dynamic-update-slice_fusion.2
  445.0 0.0 all-to-all-done.3
  445.0 6.7 all-to-all-start.5
  451.7 2.0 copy.35
  453.7 2.0 copy.34
  455.7 275.3 %all-to-all-done.5 = bf16[192,128,128]{2,1,0:T(8,128)(2,1)} async-done(((bf16[192,128,128]{2,1,0:T(8,128)(2,1)}), bf16[192,128,128]{2,1,0:T(8,128)(2,1)}, u32[]{:S(2)}, u32[]{:S(2)}) %all-to-all-start.5) | async-done | bytes 6291488 | tf_op jit(solution)/shard_map/all_to_all | solution.py:99
  731.0 4.6 convert_reduce_fusion
  (57 shorter events, 0.4 us)
Async XLA Ops:
  0.6 41.2 %copy-start = (bf16[192,4096]{1,0:T(8,128)(2,1)S(1)}, bf16[192,4096]{1,0:T(8,128)(2,1)}, u32[]{:S(2)}) copy-start(bf16[192,4096]{1,0:T(8,128)(2,1)} %param.13) | copy-start | bytes 4718596
  0.6 20.9 %copy-start.5 = (bf16[1,3,128,128]{3,2,1,0:T(8,128)(2,1)S(1)}, bf16[1,3,128,128]{3,2,1,0:T(8,128)(2,1)}, u32[]{:S(2)}) copy-start(bf16[1,3,128,128]{3,2,1,0:T(8,128)(2,1)} %param.14) | copy-start | bytes 294916
  25.7 14.9 %copy-start.6 = (s32[1,192]{1,0:T(1,128)S(1)}, s32[1,192]{1,0:T(1,128)}, u32[]{:S(2)}) copy-start(s32[1,192]{1,0:T(1,128)} %param.15) | copy-start | bytes 2308
  25.7 15.3 %copy-start.4 = (bf16[24,14336]{1,0:T(8,128)(2,1)S(1)}, bf16[24,14336]{1,0:T(8,128)(2,1)}, u32[]{:S(2)}) copy-start(bf16[24,14336]{1,0:T(8,128)(2,1)} %param.11) | copy-start | bytes 2064388
  25.7 293.4 %all-to-all-start = ((bf16[64,1,3,128,128]{4,3,2,1,0:T(8,128)(2,1)}), bf16[64,1,3,128,128]{4,3,2,1,0:T(8,128)(2,1)}, u32[]{:S(2)}, u32[]{:S(2)}) async-start(bf16[64,1,3,128,128]{4,3,2,1,0:T(8,128)(2,1)} %stack.2), calls=%async_computation | async-start | bytes 12582912 | tf_op jit(solution)/shard_map/all_to_all | solution.py:12
  41.9 1.1 copy-start.3
  319.1 57.5 %all-to-all-start.2 = ((bf16[24,8,1792]{2,0,1:T(8,128)(2,1)}), bf16[24,8,1792]{2,0,1:T(8,128)(2,1)}, u32[]{:S(2)}, u32[]{:S(2)}) async-start(bf16[24,8,1792]{2,0,1:T(8,128)(2,1)} %bitcast.111), calls=%async_computation.2 | async-start | bytes 1376256 | tf_op jit(solution)/shard_map/all_to_all | solution.py:51
  327.0 3.4 copy-start.1
  335.1 1.2 copy-start.2
  338.7 3.4 copy-start.1
  346.8 1.2 copy-start.2
  350.3 3.4 copy-start.1
  358.5 1.2 copy-start.2
  362.0 3.4 copy-start.1
  370.1 1.2 copy-start.2
  380.1 15.7 %all-to-all-start.4 = ((bf16[8,24,1792]{2,1,0:T(8,128)(2,1)}), bf16[8,24,1792]{2,1,0:T(8,128)(2,1)}, u32[]{:S(2)}, u32[]{:S(2)}) async-start(bf16[8,24,1792]{2,1,0:T(8,128)(2,1)} %get-tuple-element.173), calls=%async_computation.4 | async-start | bytes 1376256 | tf_op jit(solution)/shard_map/all_to_all | solution.py:108
  395.8 49.2 %all-to-all-start.3 = ((bf16[8,24,1792]{2,1,0:T(8,128)(2,1)}), bf16[8,24,1792]{2,1,0:T(8,128)(2,1)}, u32[]{:S(2)}, u32[]{:S(2)}) async-start(bf16[8,24,1792]{2,1,0:T(8,128)(2,1)} %get-tuple-element.174), calls=%async_computation.3 | async-start | bytes 1376256 | tf_op jit(solution)/shard_map/all_to_all | solution.py:107
  445.0 286.0 %all-to-all-start.5 = ((bf16[192,128,128]{2,1,0:T(8,128)(2,1)}), bf16[192,128,128]{2,1,0:T(8,128)(2,1)}, u32[]{:S(2)}, u32[]{:S(2)}) async-start(bf16[192,128,128]{2,1,0:T(8,128)(2,1)} %bitcast.110), calls=%async_computation.5 | async-start | bytes 12582912 | tf_op jit(solution)/shard_map/all_to_all | solution.py:99
